TPU v7x, 128 devices: a whole 4x4x4 slice. The times are simulated.
128 devices in a mesh: pts: 32 (over z, x, core), rep: 4 (over y).
Axes of the slice: x: 4, y: 4, z: 4, core: 2. Of those that a mesh axis runs over, the one named last changes fastest.
Arguments:
- target_xyz: float32 [3, 32768], P(None, 'pts'), may hold values from 0 to 1
- source_xyz: float32 [3, 65536], P(None, ('pts', 'rep')), may hold values from 0 to 1
- target_count: int32 [32], P('pts'), may hold values from 1 to 1024, as said below
- source_count: int32 [128], P(('pts', 'rep')), may hold values from 1 to 512, as said below
- psi: bfloat16 [32768, 256], P('pts'), may hold values from -6 to 6
- omega: bfloat16 [65536, 256], P(('pts', 'rep')), may hold values from -6 to 6
Outputs:
- range_sketch: float32 [32768, 256], P('pts')
- corange_sketch: float32 [65536, 256], P(('pts', 'rep'))
- core: float32 [256, 256], replicated
- range_gram: float32 [256, 256], replicated
- corange_gram: float32 [256, 256], replicated
Inputs may be any that keep to these rules, and one draw needn't show every extreme that they name: `target_count`: each group holds 1 to 1024 live targets; some group holds exactly 1024. `source_count`: each shard holds 1 to 512 live sources; some shard holds exactly 512.
All inputs are finite; a program needn't handle non-finite values.
Results may differ from a plain program's by a relative error of at most 0.0003.
The roundings to bfloat16 on the way count: a program that leaves them out, or rounds other values in their place, can miss the bound.
Values may be sent and summed in bfloat16 or wider, within the bound.
No kernel may reach another device: no remote copies, remote signals or barrier semaphores. Data moves between devices by JAX's collectives and lax.ppermute only.
A program may use at most 64 MiB of HBM per device.

v0:
```python
import math
import jax
import jax.numpy as jnp
from jax import lax
from jax.sharding import PartitionSpec as P

SHIFT = 1.05
SPREAD = 8.0


def tile_block(tgt, src):
    dx = tgt[0][:, None] - (src[0][None, :] + SHIFT)
    dy = SPREAD * (tgt[1][:, None] - src[1][None, :])
    dz = SPREAD * (tgt[2][:, None] - src[2][None, :])
    return lax.rsqrt(dx * dx + dy * dy + dz * dz).astype(jnp.bfloat16)


def local(target_xyz, source_xyz, target_count, source_count, psi, omega):
    tcap = psi.shape[0]
    scap = omega.shape[0]
    width = psi.shape[1]
    n_pts = lax.axis_size("pts")
    n_rep = lax.axis_size("rep")
    all_targets = tcap * n_pts
    all_sources = scap * n_pts * n_rep
    tlive = jnp.arange(tcap, dtype=jnp.int32) < target_count[0]
    slive = jnp.arange(scap, dtype=jnp.int32) < source_count[0]
    psi_live = jnp.where(tlive[:, None], psi, jnp.zeros_like(psi))
    omega_live = jnp.where(slive[:, None], omega, jnp.zeros_like(omega))
    hi = lax.Precision.HIGHEST
    src_all = lax.all_gather(source_xyz, "pts", axis=1, tiled=True)
    piece = lax.all_gather(omega_live, "pts", axis=0, tiled=True)

    def range_inner(j, acc):
        rows = lax.dynamic_slice_in_dim(piece, j * scap, scap, 0)
        where = lax.dynamic_slice_in_dim(src_all, j * scap, scap, 1)
        return acc + jnp.dot(
            tile_block(target_xyz, where), rows, preferred_element_type=jnp.float32
        )

    y_part = lax.fori_loop(
        0, piece.shape[0] // scap, range_inner, jnp.zeros((tcap, width), jnp.float32)
    )
    y_sum = lax.psum(y_part, "rep") * (2.0 / math.sqrt(all_sources))
    range_sketch = jnp.where(tlive[:, None], y_sum, jnp.zeros_like(y_sum))
    tgt_all = lax.all_gather(target_xyz, "pts", axis=1, tiled=True)
    corange_piece = lax.all_gather(psi_live, "pts", axis=0, tiled=True)

    def corange_inner(j, acc):
        rows = lax.dynamic_slice_in_dim(corange_piece, j * tcap, tcap, 0)
        where = lax.dynamic_slice_in_dim(tgt_all, j * tcap, tcap, 1)
        tile = tile_block(where, source_xyz)
        return acc + lax.dot_general(
            tile, rows, (((0,), (0,)), ((), ())), preferred_element_type=jnp.float32
        )

    z_sum = lax.fori_loop(
        0, corange_piece.shape[0] // tcap, corange_inner, jnp.zeros((scap, width), jnp.float32)
    )
    z_scaled = z_sum * (2.0 / math.sqrt(all_targets))
    corange_sketch = jnp.where(slive[:, None], z_scaled, jnp.zeros_like(z_scaled))
    z_gram_part = jnp.dot(corange_sketch.T, corange_sketch, precision=hi)
    core_part = jnp.dot(psi_live.astype(jnp.float32).T, range_sketch, precision=hi)
    y_gram_part = jnp.dot(range_sketch.T, range_sketch, precision=hi)
    core_sum, y_gram = lax.psum((core_part, y_gram_part), "pts")
    z_gram = lax.psum(z_gram_part, ("pts", "rep"))
    core = core_sum / math.sqrt(all_targets)
    range_gram = y_gram / all_targets
    corange_gram = z_gram / all_sources
    return (range_sketch, corange_sketch, core, range_gram, corange_gram)


def solution(mesh):
    return jax.shard_map(
        local,
        mesh=mesh,
        in_specs=(
            P(None, "pts"),
            P(None, ("pts", "rep")),
            P("pts"),
            P(("pts", "rep")),
            P("pts", None),
            P(("pts", "rep"), None),
        ),
        out_specs=(P("pts", None), P(("pts", "rep"), None), P(), P(), P()),
        check_vma=False,
    )
```

profile of v0, /device:TPU:1, one launch (start us, length us, event | category | flops | bytes accessed | tf_op | source)
XLA Modules:
  0.0 550.0 jit_solution(14603858195827019406)
XLA Ops:
  9.7 27.6 %all_gather.12 = f32[3,16384]{1,0:T(4,128)S(1)} all-gather(f32[3,512]{1,0:T(4,128)} %param.11), channel_id=1, replica_groups=mesh['pts'=32,'rep'=4] {'pts'}, dimensions={1}, use_global_device_ids=true | all-gather | bytes 202752 | tf_op jit(solution)/shard_map/all_gather | solution.py:31
  37.3 30.2 %all-gather.3.cloned.1.call-done = bf16[16384,256]{1,0:T(8,128)(2,1)} async-done(((bf16[512,256]{1,0:T(8,128)(2,1)}), bf16[16384,256]{1,0:T(8,128)(2,1)}) %all-gather.3.cloned.1.call-update) | async-done | bytes 8388624 | tf_op jit(solution)/shard_map/all_gather | solution.py:32
  67.5 96.4 %while.28 = (s32[]{:T(128)}, f32[1024,256]{1,0:T(8,128)S(1)}, f32[3,1024]{1,0:T(4,128)}, f32[3,16384]{1,0:T(4,128)S(1)}, bf16[16384,256]{1,0:T(8,128)(2,1)}, /*i...) while((s32[]{:T(128)}, f32[1024,256]{1,0:T(8,128)S(1)}, ...), condition=%wide.region_1.2_spmd.clone, body=%wide.region_0.1_spmd.clone.sunk | while | flops 274727424 | bytes 2414797 | solution.py:41
  166.7 24.7 %all_gather.14 = f32[3,32768]{1,0:T(4,128)S(1)} all-gather(f32[3,1024]{1,0:T(4,128)S(1)} %copy-done.5), channel_id=1, replica_groups=mesh['pts'=32,'rep'=4] {'pts'}, dimensions={1}, use_global_device_ids=true | all-gather | bytes 405504 | tf_op jit(solution)/shard_map/all_gather | solution.py:46
  191.4 17.0 %all-reduce.5.cloned.1.call-done = f32[1024,256]{1,0:T(8,128)} async-done(((f32[1024,256]{1,0:T(8,128)}), f32[1024,256]{1,0:T(8,128)}) %all-reduce.5.cloned.1.call-update) | async-done | bytes 1048592 | tf_op jit(solution)/shard_map/psum | solution.py:44
  211.4 2.6 fusion.22
  214.0 73.1 %all-gather.5.cloned.1.call-done = bf16[32768,256]{1,0:T(8,128)(2,1)} async-done(((bf16[1024,256]{1,0:T(8,128)(2,1)}), bf16[32768,256]{1,0:T(8,128)(2,1)}) %all-gather.5.cloned.1.call-update) | async-done | bytes 16777232 | tf_op jit(solution)/shard_map/all_gather | solution.py:47
  287.1 81.4 %while.29 = (s32[]{:T(128)}, f32[512,256]{1,0:T(8,128)S(1)}, f32[3,32768]{1,0:T(4,128)S(1)}, f32[3,512]{1,0:T(4,128)S(1)}, bf16[32768,256]{1,0:T(8,128)(2,1)}, /...) while((s32[]{:T(128)}, f32[512,256]{1,0:T(8,128)S(1)}, ...), condition=%wide.region_4.5_spmd.clone, body=%wide.region_3.4_spmd.clone.sunk | while | flops 274465280 | bytes 1628365 | solution.py:57
  287.2 2.4 convolution_add_fusion.5
  289.8 2.4 convolution_add_fusion.5
  292.3 2.4 convolution_add_fusion.5
  294.8 2.4 convolution_add_fusion.5
  297.4 2.4 convolution_add_fusion.5
  300.0 2.4 convolution_add_fusion.5
  302.5 2.4 convolution_add_fusion.5
  305.0 2.4 convolution_add_fusion.5
  315.2 2.4 convolution_add_fusion.5
  317.8 2.4 convolution_add_fusion.5
  320.3 2.4 convolution_add_fusion.5
  322.9 2.4 convolution_add_fusion.5
  325.4 2.4 convolution_add_fusion.5
  327.9 2.4 convolution_add_fusion.5
  333.0 2.4 convolution_add_fusion.5
  335.6 2.4 convolution_add_fusion.5
  338.1 2.4 convolution_add_fusion.5
  348.3 2.4 convolution_add_fusion.5
  350.9 2.4 convolution_add_fusion.5
  355.9 2.4 convolution_add_fusion.5
  358.5 2.4 convolution_add_fusion.5
  361.0 2.4 convolution_add_fusion.5
  370.5 24.1 %all-reduce.9.cloned.1.call-done = (f32[256,256]{1,0:T(8,128)}, f32[256,256]{1,0:T(8,128)}) async-done(((f32[256,256]{1,0:T(8,128)}, f32[256,256]{1,0:T(8,128)}), (f32[256,256]{1,0:T(8,128)}, f32[256,256]{1,0:T(8,128)})) %all-reduce.9.cloned.1.call-update) | async-done | bytes 524304 | tf_op jit(solution)/shard_map/psum | solution.py:65
  396.4 145.4 %all-reduce.7.cloned.1.call-done = f32[256,256]{1,0:T(8,128)} async-done(((f32[256,256]{1,0:T(8,128)}), f32[256,256]{1,0:T(8,128)}) %all-reduce.7.cloned.1.call-update) | async-done | bytes 262160 | tf_op jit(solution)/shard_map/psum | solution.py:66
  (206 shorter events, 134.8 us)
Async XLA Ops:
  7.2 60.3 %all-gather.3.cloned.1.call-start = ((), (), s32[]{:S(2)}) async-start(), calls=%async_computation | async-start | bytes 8650752 | tf_op jit(solution)/shard_map/all_gather | solution.py:32
  9.7 198.7 %all-reduce.5.cloned.1.call-start = ((), (), s32[]{:S(2)}) async-start(), calls=%async_computation.1 | async-start | bytes 2097152 | tf_op jit(solution)/shard_map/psum | solution.py:44
  67.5 98.1 %copy-start.4 = (bf16[1024,256]{1,0:T(8,128)(2,1)S(1)}, bf16[1024,256]{1,0:T(8,128)(2,1)}, u32[]{:S(2)}) copy-start(bf16[1024,256]{1,0:T(8,128)(2,1)} %param.14) | copy-start | bytes 1572868
  163.9 1.0 copy-start.3
  163.9 2.8 copy-start.5
  164.9 122.2 %all-gather.5.cloned.1.call-start = ((), (), s32[]{:S(2)}) async-start(), calls=%async_computation.2 | async-start | bytes 17301504 | tf_op jit(solution)/shard_map/all_gather | solution.py:47
  166.6 43.2 %copy-start.2 = (bf16[1024,256]{1,0:T(8,128)(2,1)S(1)}, bf16[1024,256]{1,0:T(8,128)(2,1)}, u32[]{:S(2)}) copy-start(bf16[1024,256]{1,0:T(8,128)(2,1)} %broadcast_select_fusion) | copy-start | bytes 1572868
  166.6 227.9 %all-reduce.9.cloned.1.call-start = ((), (), s32[]{:S(2)}) async-start(), calls=%async_computation.4 | async-start | bytes 1048576 | tf_op jit(solution)/shard_map/psum | solution.py:65
  209.8 4.1 copy-start
  209.9 77.3 %copy-start.6 = (f32[3,512]{1,0:T(4,128)S(1)}, f32[3,512]{1,0:T(4,128)}, u32[]{:S(2)}) copy-start(f32[3,512]{1,0:T(4,128)} %param.11) | copy-start | bytes 18436
  214.0 327.8 %all-reduce.7.cloned.1.call-start = ((), (), s32[]{:S(2)}) async-start(), calls=%async_computation.3 | async-start | bytes 524288 | tf_op jit(solution)/shard_map/psum | solution.py:66
  368.7 174.8 %copy-start.1 = (f32[512,256]{1,0:T(8,128)}, f32[512,256]{1,0:T(8,128)S(1)}, u32[]{:S(2)}) copy-start(f32[512,256]{1,0:T(8,128)S(1)} %multiply_select_fusion.1) | copy-start | bytes 1572868
Sparse Core Ops, SparseCore 0:
  10.8 56.6 all-gather.2
  165.0 43.3 all-reduce.4
  211.2 75.8 all-gather.4
  290.8 103.6 all-reduce.8
  399.1 142.5 all-reduce.6
where the time goes:
time: 555 us; the launch traced here: 550 us
  waiting for transfers between devices  290 us (52%)
  matrix products  148 us (27%)
  blocking collectives  52.2 us (9%)
  local copies, waits for them, and re-layouts  30.9 us (6%)
  between operations  15.2 us (3%)
  other arithmetic  10.8 us (2%)
    psum x1, waiting for transfers between devices, local(): z_gram = lax.psum(z_gram_part, ('pts', 'rep'))  145 us
    dot_general x32, matrix products, corange_inner(): lax.dot_general(tile, rows, (((0,), (0,)), ((), ())), preferred_element_t...  76.9 us
    all_gather x1, waiting for transfers between devices, local(): corange_piece = lax.all_gather(psi_live, 'pts', axis=0, tiled=True)  73.1 us
    dot_general x32, matrix products, range_inner(): jnp.dot(tile_block(target_xyz, where), rows, preferred_element_type=jnp.f...  65.5 us
    all_gather x1, waiting for transfers between devices, local(): piece = lax.all_gather(omega_live, 'pts', axis=0, tiled=True)  30.2 us
    slice x64, local copies, waits for them, and re-layouts, tile_block(): dx = tgt[0][:, None] - (src[0][None, :] + SHIFT)  30 us
    all_gather x1, blocking collectives, local(): src_all = lax.all_gather(source_xyz, 'pts', axis=1, tiled=True)  27.6 us
    all_gather x1, blocking collectives, local(): tgt_all = lax.all_gather(target_xyz, 'pts', axis=1, tiled=True)  24.7 us
  transfers between devices with their start and end apart: 5, of which 5 were waited for; matrix products, arithmetic and copies ran while one was open for 16% of the time, Pallas kernels for 0%

commit v1 on v0

--- a/solution.py
+++ b/solution.py
@@ -63,7 +63,7 @@
     core_part = jnp.dot(psi_live.astype(jnp.float32).T, range_sketch, precision=hi)
     y_gram_part = jnp.dot(range_sketch.T, range_sketch, precision=hi)
     core_sum, y_gram = lax.psum((core_part, y_gram_part), "pts")
-    z_gram = lax.psum(z_gram_part, ("pts", "rep"))
+    z_gram = lax.psum(lax.psum(z_gram_part, "rep"), "pts")
     core = core_sum / math.sqrt(all_targets)
     range_gram = y_gram / all_targets
     corange_gram = z_gram / all_sources

time: 555 us -> 397 us (0.72)
  waiting for transfers between devices: 290 us -> 160 us
  local copies, waits for them, and re-layouts: 30.9 us -> 3.21 us
    psum x1 -> x0, waiting for transfers between devices: 145 us -> none  [local(): z_gram = lax.psum(z_gram_part, ('pts', 'rep'))]
    psum x1, waiting for transfers between devices: 24.1 us -> 106 us  [local(): core_sum, y_gram = lax.psum((core_part, y_gram_part), 'pts')]
    all_gather x1, waiting for transfers between devices: 73.1 us -> 4.8 us  [local(): corange_piece = lax.all_gather(psi_live, 'pts', axis=0, tiled=True)]
    psum x1, waiting for transfers between devices: 17 us -> 45.7 us  [local(): y_sum = lax.psum(y_part, 'rep') * (2.0 / math.sqrt(all_sources))]
    all_gather x1, waiting for transfers between devices: 30.2 us -> 3.39 us  [local(): piece = lax.all_gather(omega_live, 'pts', axis=0, tiled=True)]
    slice x64, local copies, waits for them, and re-layouts: 30 us -> 3.18 us  [tile_block(): dx = tgt[0][:, None] - (src[0][None, :] + SHIFT)]
  transfers between devices with their start and end apart: 5 -> 4, of which waited for: 5 -> 4; matrix products, arithmetic and copies ran while one was open for 16% -> 18% of each run, Pallas kernels for 0% -> 0%
where the time goes in v1:
time: 397 us; the launch traced here: 394 us
  waiting for transfers between devices  160 us (40%)
  matrix products  148 us (37%)
  blocking collectives  52.6 us (13%)
  between operations  15.2 us (4%)
  other arithmetic  11.9 us (3%)
    psum x1, waiting for transfers between devices, local(): core_sum, y_gram = lax.psum((core_part, y_gram_part), 'pts')  106 us
    dot_general x32, matrix products, corange_inner(): lax.dot_general(tile, rows, (((0,), (0,)), ((), ())), preferred_element_t...  76.8 us
    dot_general x32, matrix products, range_inner(): jnp.dot(tile_block(target_xyz, where), rows, preferred_element_type=jnp.f...  65.4 us
    psum x1, waiting for transfers between devices, local(): y_sum = lax.psum(y_part, 'rep') * (2.0 / math.sqrt(all_sources))  45.7 us
    all_gather x1, blocking collectives, local(): src_all = lax.all_gather(source_xyz, 'pts', axis=1, tiled=True)  27.6 us
    all_gather x1, blocking collectives, local(): tgt_all = lax.all_gather(target_xyz, 'pts', axis=1, tiled=True)  25 us
  transfers between devices with their start and end apart: 4, of which 4 were waited for; matrix products, arithmetic and copies ran while one was open for 18% of the time, Pallas kernels for 0%

profile of v1, /device:TPU:1, one launch (start us, length us, event | category | flops | bytes accessed | tf_op | source)
XLA Modules:
  0.0 393.8 jit_solution(6929666012026541603)
XLA Ops:
  12.6 27.6 %all_gather.12 = f32[3,16384]{1,0:T(4,128)S(1)} all-gather(f32[3,512]{1,0:T(4,128)S(1)} %copy-done.5), channel_id=1, replica_groups=mesh['pts'=32,'rep'=4] {'pts'}, dimensions={1}, use_global_device_ids=true | all-gather | bytes 202752 | tf_op jit(solution)/shard_map/all_gather | solution.py:31
  40.2 25.0 %all_gather.14 = f32[3,32768]{1,0:T(4,128)S(1)} all-gather(f32[3,1024]{1,0:T(4,128)S(1)} %copy-done.4), channel_id=1, replica_groups=mesh['pts'=32,'rep'=4] {'pts'}, dimensions={1}, use_global_device_ids=true | all-gather | bytes 405504 | tf_op jit(solution)/shard_map/all_gather | solution.py:46
  65.2 3.4 all-gather.3.cloned.1.call-done
  68.6 69.7 %while.28 = (s32[]{:T(128)}, f32[1024,256]{1,0:T(8,128)S(1)}, f32[3,1024]{1,0:T(4,128)S(1)}, f32[3,16384]{1,0:T(4,128)S(1)}, bf16[16384,256]{1,0:T(8,128)(2,1)},...) while((s32[]{:T(128)}, f32[1024,256]{1,0:T(8,128)S(1)}, ...), condition=%wide.region_1.2_spmd.clone, body=%wide.region_0.1_spmd.clone.sunk | while | flops 274727424 | bytes 2414797 | solution.py:41
  138.3 4.8 %all-gather.5.cloned.1.call-done = bf16[32768,256]{1,0:T(8,128)(2,1)} async-done(((bf16[1024,256]{1,0:T(8,128)(2,1)}), bf16[32768,256]{1,0:T(8,128)(2,1)}) %all-gather.5.cloned.1.call-update) | async-done | bytes 16777232 | tf_op jit(solution)/shard_map/all_gather | solution.py:47
  143.1 81.2 %while.29 = (s32[]{:T(128)}, f32[512,256]{1,0:T(8,128)S(1)}, f32[3,32768]{1,0:T(4,128)S(1)}, f32[3,512]{1,0:T(4,128)S(1)}, bf16[32768,256]{1,0:T(8,128)(2,1)}, /...) while((s32[]{:T(128)}, f32[512,256]{1,0:T(8,128)S(1)}, ...), condition=%wide.region_4.5_spmd.clone, body=%wide.region_3.4_spmd.clone.sunk | while | flops 274465280 | bytes 1628365 | solution.py:57
  143.2 2.4 convolution_add_fusion.5
  145.7 2.4 convolution_add_fusion.5
  148.3 2.4 convolution_add_fusion.5
  150.8 2.4 convolution_add_fusion.5
  153.4 2.4 convolution_add_fusion.5
  158.4 2.4 convolution_add_fusion.5
  161.0 2.4 convolution_add_fusion.5
  163.5 2.4 convolution_add_fusion.5
  166.1 2.4 convolution_add_fusion.5
  168.6 2.4 convolution_add_fusion.5
  173.7 2.4 convolution_add_fusion.5
  178.8 2.4 convolution_add_fusion.5
  181.3 2.4 convolution_add_fusion.5
  183.8 2.4 convolution_add_fusion.5
  188.9 2.4 convolution_add_fusion.5
  194.0 2.4 convolution_add_fusion.5
  199.1 2.4 convolution_add_fusion.5
  201.6 2.4 convolution_add_fusion.5
  204.1 2.4 convolution_add_fusion.5
  209.2 2.4 convolution_add_fusion.5
  214.3 2.4 convolution_add_fusion.5
  219.4 2.4 convolution_add_fusion.5
  221.9 2.4 convolution_add_fusion.5
  226.3 45.7 %all-reduce.7.cloned.1.call-done = (f32[1024,256]{1,0:T(8,128)}, f32[256,256]{1,0:T(8,128)}) async-done(((f32[1024,256]{1,0:T(8,128)}, f32[256,256]{1,0:T(8,128)}), (f32[1024,256]{1,0:T(8,128)}, f32[256,256]{1,0:T(8,128)})) %all-reduce.7.cloned.1.call-update) | async-done | bytes 1310736 | tf_op jit(solution)/shard_map/psum | solution.py:44
  275.0 2.5 fusion.22
  277.5 106.3 %all-reduce.5.cloned.1.call-done = (f32[256,256]{1,0:T(8,128)}, f32[256,256]{1,0:T(8,128)}, f32[256,256]{1,0:T(8,128)}) async-done(((f32[256,256]{1,0:T(8,128)}, f32[256,256]{1,0:T(8,128)}, f32[256,256]{1,0:T(8,128)}), (f32[256,256]{1,0:T(8,128)}, f32[256,256]{1,0:T(8,128)}, f32[256,256]{1,0:T(8,128)})) %all-reduce.5.cloned.1.call-update) | async-done | bytes 786448 | tf_op jit(solution)/shard_map/psum | solution.py:65
  (201 shorter events, 105.6 us)
Async XLA Ops:
  7.2 5.4 %copy-start.5 = (f32[3,512]{1,0:T(4,128)S(1)}, f32[3,512]{1,0:T(4,128)}, u32[]{:S(2)}) copy-start(f32[3,512]{1,0:T(4,128)} %param.11) | copy-start | bytes 18436
  7.2 33.0 %copy-start.4 = (f32[3,1024]{1,0:T(4,128)S(1)}, f32[3,1024]{1,0:T(4,128)}, u32[]{:S(2)}) copy-start(f32[3,1024]{1,0:T(4,128)} %param.10) | copy-start | bytes 36868
  7.2 61.4 %all-gather.3.cloned.1.call-start = ((), (), s32[]{:S(2)}) async-start(), calls=%async_computation | async-start | bytes 8650752 | tf_op jit(solution)/shard_map/all_gather | solution.py:32
  9.7 133.4 %all-gather.5.cloned.1.call-start = ((), (), s32[]{:S(2)}) async-start(), calls=%async_computation.1 | async-start | bytes 17301504 | tf_op jit(solution)/shard_map/all_gather | solution.py:47
  12.5 259.5 %all-reduce.7.cloned.1.call-start = ((), (), s32[]{:S(2)}) async-start(), calls=%async_computation.3 | async-start | bytes 2621440 | tf_op jit(solution)/shard_map/psum | solution.py:44
  138.3 4.8 %copy-start.3 = (f32[1024,256]{1,0:T(8,128)}, f32[1024,256]{1,0:T(8,128)S(1)}, u32[]{:S(2)}) copy-start(f32[1024,256]{1,0:T(8,128)S(1)} %get-tuple-element.193) | copy-start | bytes 3145732
  224.5 49.0 %copy-start.2 = (f32[512,256]{1,0:T(8,128)}, f32[512,256]{1,0:T(8,128)S(1)}, u32[]{:S(2)}) copy-start(f32[512,256]{1,0:T(8,128)S(1)} %multiply_select_fusion.1) | copy-start | bytes 1572868
  224.5 49.0 %copy-start.1 = (bf16[1024,256]{1,0:T(8,128)(2,1)S(1)}, bf16[1024,256]{1,0:T(8,128)(2,1)}, u32[]{:S(2)}) copy-start(bf16[1024,256]{1,0:T(8,128)(2,1)} %broadcast_select_fusion) | copy-start | bytes 1572868
  226.2 157.5 %all-reduce.5.cloned.1.call-start = ((), (), s32[]{:S(2)}) async-start(), calls=%async_computation.2 | async-start | bytes 1572864 | tf_op jit(solution)/shard_map/psum | solution.py:65
  273.4 4.1 %copy-start = (f32[1024,256]{1,0:T(8,128)}, f32[1024,256]{1,0:T(8,128)S(1)}, u32[]{:S(2)}) copy-start(f32[1024,256]{1,0:T(8,128)S(1)} %multiply_select_fusion) | copy-start | bytes 3145732
Sparse Core Ops, SparseCore 0:
  10.8 57.6 all-gather.2
  70.8 72.2 all-gather.4
  226.4 45.5 all-reduce.6
  277.6 106.0 all-reduce.4
